TPU v7x, 256 devices: a whole 4x4x8 slice. The times are simulated.
256 devices in a mesh: dp: 2 (over core), expert: 128 (over y, x, z).
Axes of the slice: x: 4, y: 4, z: 8, core: 2. Of those that a mesh axis runs over, the one named last changes fastest.
Arguments:
- tokens: bfloat16 [32768, 2048], P(('dp', 'expert')), parts along dimension 0, may hold values from -6 to 6
- cotangent: bfloat16 [32768, 2048], P(('dp', 'expert')), parts along dimension 0, may hold values from -6 to 6
- expert_ids: int32 [32768, 10], P(('dp', 'expert')), parts along dimension 0, may hold values from 0 to 255, all different within a row; in each aligned block of 128 rows (0 to 127, 128 to 255, ...) at most 6 rows name the same one
- probs: float32 [32768, 10], P(('dp', 'expert')), parts along dimension 0, may hold values from 0.05 to 0.5
- gate_weight: bfloat16 [512, 2048, 256], P(('dp', 'expert')), parts along dimension 0, may hold values from -0.125 to 0.125
- up_weight: bfloat16 [512, 2048, 256], P(('dp', 'expert')), parts along dimension 0, may hold values from -0.125 to 0.125
- down_weight: bfloat16 [512, 256, 2048], P(('dp', 'expert')), parts along dimension 0, may hold values from -0.375 to 0.375
Outputs:
- mixed: float32 [32768, 2048], P(('dp', 'expert')), parts along dimension 0
- input_grad: float32 [32768, 2048], P(('dp', 'expert')), parts along dimension 0
There are 2 independent parts, one for each index of `dp`. A program takes and returns all parts, laid end to end along the dimension named above; each array names one. Nothing has to cross between parts.
Inputs may be any that keep to these rules, and one draw needn't show every extreme that they name: `expert_ids`: each row names 10 different experts. Within the 128 rows of one device no expert is named by more than 6 rows, and in some of these blocks one expert is named by exactly 6 rows; loads across experts are skewed.
All inputs are finite; a program needn't handle non-finite values.
Results may differ from a plain program's by a relative error of at most 0.0041.
Values may be sent and summed in bfloat16 or wider, within the bound.
A program may use at most 128 MiB of HBM per device.

v0:
```python
import jax
import jax.numpy as jnp
from jax import lax
from jax.sharding import PartitionSpec as P


def route_slots(expert_ids, local_count, device_count, capacity):
    experts = local_count * device_count
    row_count = expert_ids.shape[0] * expert_ids.shape[1]
    flat_ids = expert_ids.reshape(row_count)
    sort_order = jnp.argsort(flat_ids, stable=True)
    labels = lax.broadcasted_iota(jnp.int32, (1, experts), 1)
    counts = jnp.sum((flat_ids[:, None] == labels).astype(jnp.int32), axis=0)
    starts = jnp.cumsum(counts) - counts
    sorted_ids = flat_ids[sort_order]
    rank_within = jnp.arange(row_count, dtype=jnp.int32) - starts[sorted_ids]
    owner = sorted_ids // local_count
    local_slot = sorted_ids % local_count
    target = local_slot * (device_count * capacity) + owner * capacity + rank_within
    source_of = jnp.full((experts * capacity,), row_count, jnp.int32).at[target].set(sort_order)
    target_of = jnp.zeros((row_count,), jnp.int32).at[sort_order].set(target)
    return (source_of, target_of)


def pack_rows(values, source_of, top_count, local_count):
    token_count = values.shape[0]
    with_zero = jnp.concatenate([values, jnp.zeros((1, values.shape[1]), values.dtype)], axis=0)
    token_index = jnp.minimum(source_of // top_count, token_count)
    picked = with_zero[token_index]
    return picked.reshape(local_count, -1, values.shape[1])


def forward_part(received, gate_weight, up_weight, down_weight):
    gate_pre = jnp.einsum("erd,edh->erh", received, gate_weight, preferred_element_type=jnp.float32)
    up_pre = jnp.einsum("erd,edh->erh", received, up_weight, preferred_element_type=jnp.float32)
    sigmoid_gate = jax.nn.sigmoid(gate_pre)
    activ = (gate_pre * sigmoid_gate * up_pre).astype(jnp.bfloat16)
    expert_out = jnp.einsum("erh,ehd->erd", activ, down_weight, preferred_element_type=jnp.float32)
    return (expert_out.astype(jnp.bfloat16), gate_pre, up_pre, sigmoid_gate)


def backward_part(grad_rows, gate_pre, up_pre, sigmoid_gate, gate_weight, up_weight, down_weight):
    grad_act = jnp.einsum(
        "erd,ehd->erh", grad_rows, down_weight, preferred_element_type=jnp.float32
    )
    grad_gate = (grad_act * up_pre * sigmoid_gate * (1.0 + gate_pre * (1.0 - sigmoid_gate))).astype(
        jnp.bfloat16
    )
    grad_up = (grad_act * gate_pre * sigmoid_gate).astype(jnp.bfloat16)
    joined_grad = jnp.concatenate([grad_gate, grad_up], axis=2)
    joined_weight = jnp.concatenate([gate_weight, up_weight], axis=2)
    expert_back = jnp.einsum(
        "erh,edh->erd", joined_grad, joined_weight, preferred_element_type=jnp.float32
    )
    return expert_back.astype(jnp.bfloat16)


def combine_rows(returned, target_of, probs):
    token_count, top_count = probs.shape
    flat_back = returned.reshape(-1, returned.shape[2])
    picked = flat_back[target_of].reshape(token_count, top_count, returned.shape[2])
    return jnp.sum(picked.astype(jnp.float32) * probs[:, :, None], axis=1)


def on_device(tokens, cotangent, expert_ids, probs, gate_weight, up_weight, down_weight):
    local_count = gate_weight.shape[0]
    device_count = lax.axis_size("expert")
    experts = local_count * device_count
    token_count, top_count = expert_ids.shape
    row_count = token_count * top_count
    capacity = row_count * 6 // (5 * experts)
    source_of, target_of = route_slots(expert_ids, local_count, device_count, capacity)
    send_rows = pack_rows(tokens, source_of, top_count, local_count)
    send_grads = pack_rows(cotangent, source_of, top_count, local_count)
    received = lax.all_to_all(send_rows, "expert", split_axis=1, concat_axis=1, tiled=True)
    expert_out, gate_pre, up_pre, sigmoid_gate = forward_part(
        received, gate_weight, up_weight, down_weight
    )
    returned_out = lax.all_to_all(expert_out, "expert", split_axis=1, concat_axis=1, tiled=True)
    received_grads = lax.all_to_all(send_grads, "expert", split_axis=1, concat_axis=1, tiled=True)
    expert_back = backward_part(
        received_grads, gate_pre, up_pre, sigmoid_gate, gate_weight, up_weight, down_weight
    )
    returned_back = lax.all_to_all(expert_back, "expert", split_axis=1, concat_axis=1, tiled=True)
    mixed = combine_rows(returned_out, target_of, probs)
    input_grad = combine_rows(returned_back, target_of, probs)
    return (mixed, input_grad)


def solution(mesh):
    in_specs = (
        P(("dp", "expert"), None),
        P(("dp", "expert"), None),
        P(("dp", "expert"), None),
        P(("dp", "expert"), None),
        P(("dp", "expert"), None, None),
        P(("dp", "expert"), None, None),
        P(("dp", "expert"), None, None),
    )
    out_specs = (P(("dp", "expert"), None), P(("dp", "expert"), None))
    return jax.shard_map(
        on_device, mesh=mesh, in_specs=in_specs, out_specs=out_specs, check_vma=False
    )
```

profile of v0, /device:TPU:32, one launch (start us, length us, event | category | flops | bytes accessed | tf_op | source)
XLA Modules:
  0.0 731.4 jit_solution(8434159250508726755)
XLA Ops:
  0.6 0.0 copy-start
  0.6 0.9 copy.35
  1.6 0.1 reshape.151
  1.7 0.3 convert_reduce_fusion
  2.0 0.3 reduce-window.9
  2.3 0.1 slice.7
  2.4 0.1 slice_reduce_fusion
  2.5 0.1 bitcast_subtract_fusion
  2.6 5.0 sort.17
  7.7 7.1 gather_fusion
  14.8 0.0 copy-start.2
  14.8 7.9 %gather_fusion.1 = s32[1280]{0:T(1024)S(1)} fusion(s32[256]{0:T(256)S(1)} %bitcast_subtract_fusion, s32[2048]{0:T(1024)S(1)} %pad_clamp_fusion.2), kind=kCustom, calls=%fused_computation.1 | custom fusion | bytes 15360 | tf_op jit(solution)/shard_map/gather | solution.py:16
  22.8 0.1 fusion.24
  22.8 5.2 scatter_custom_fusion
  28.1 0.0 copy-done.2
  28.2 7.1 gather_fusion.2
  35.3 12.6 %copy.36 = bf16[2,768,2048]{2,0,1:T(2,128)(2,1)} copy(bf16[2,768,2048]{2,1,0:T(8,128)(2,1)} %bitcast.14) | data formatting | bytes 12582912 | tf_op jit(solution)/shard_map/reshape | solution.py:30
  47.9 15.5 %all-to-all-start = ((bf16[2,768,2048]{2,0,1:T(2,128)(2,1)}), bf16[2,768,2048]{2,0,1:T(2,128)(2,1)}, u32[]{:S(2)}, u32[]{:S(2)}) async-start(bf16[2,768,2048]{2,0,1:T(2,128)(2,1)} %copy.36), calls=%async_computation | async-start | bytes 12582912 | tf_op jit(solution)/shard_map/all_to_all | solution.py:75
  63.5 0.0 copy-done.3
  63.5 7.0 gather_fusion.4
  70.6 12.6 %copy.45 = bf16[2,768,2048]{2,0,1:T(2,128)(2,1)} copy(bf16[2,768,2048]{2,1,0:T(8,128)(2,1)} %bitcast.13) | data formatting | bytes 12582912 | tf_op jit(solution)/shard_map/reshape | solution.py:30
  83.2 123.7 %all-to-all-done = bf16[2,768,2048]{2,0,1:T(2,128)(2,1)} async-done(((bf16[2,768,2048]{2,0,1:T(2,128)(2,1)}), bf16[2,768,2048]{2,0,1:T(2,128)(2,1)}, u32[]{:S(2)}, u32[]{:S(2)}) %all-to-all-start) | async-done | bytes 6291488 | tf_op jit(solution)/shard_map/all_to_all | solution.py:75
  206.9 8.1 %all-to-all-start.2 = ((bf16[2,768,2048]{2,0,1:T(2,128)(2,1)}), bf16[2,768,2048]{2,0,1:T(2,128)(2,1)}, u32[]{:S(2)}, u32[]{:S(2)}) async-start(bf16[2,768,2048]{2,0,1:T(2,128)(2,1)} %copy.45), calls=%async_computation.2 | async-start | bytes 12582912 | tf_op jit(solution)/shard_map/all_to_all | solution.py:80
  215.0 6.9 fusion.2
  221.9 133.6 %all-to-all-done.2 = bf16[2,768,2048]{2,0,1:T(2,128)(2,1)} async-done(((bf16[2,768,2048]{2,0,1:T(2,128)(2,1)}), bf16[2,768,2048]{2,0,1:T(2,128)(2,1)}, u32[]{:S(2)}, u32[]{:S(2)}) %all-to-all-start.2) | async-done | bytes 6291488 | tf_op jit(solution)/shard_map/all_to_all | solution.py:80
  355.6 0.0 copy-done
  355.6 7.2 fusion
  362.8 0.0 copy-done.6
  362.8 0.0 copy-done.7
  362.8 6.7 multiply_convert_fusion.1
  369.6 2.0 convolution_convert_fusion.1
  371.5 19.2 %copy.42 = bf16[2,768,2048]{2,0,1:T(2,128)(2,1)} copy(bf16[2,768,2048]{2,1,0:T(8,128)(2,1)S(1)} %convolution_convert_fusion.1) | data formatting | bytes 12582912 | tf_op jit(solution)/shard_map/convert_element_type | solution.py:39
  390.7 7.0 all-to-all-start.1
  397.7 0.0 copy-done.5
  397.7 5.5 convolution_convert_fusion
  403.2 18.8 %copy.48 = bf16[2,768,2048]{2,0,1:T(2,128)(2,1)} copy(bf16[2,768,2048]{2,1,0:T(8,128)(2,1)S(1)} %convolution_convert_fusion) | data formatting | bytes 12582912 | tf_op jit(solution)/shard_map/convert_element_type | solution.py:55
  422.0 115.3 %all-to-all-done.1 = bf16[2,768,2048]{2,0,1:T(2,128)(2,1)} async-done(((bf16[2,768,2048]{2,0,1:T(2,128)(2,1)}), bf16[2,768,2048]{2,0,1:T(2,128)(2,1)}, u32[]{:S(2)}, u32[]{:S(2)}) %all-to-all-start.1) | async-done | bytes 6291488 | tf_op jit(solution)/shard_map/all_to_all | solution.py:79
  537.3 7.2 all-to-all-start.3
  544.6 5.4 scatter_custom_fusion.1
  550.0 0.1 copy.44
  550.1 8.3 %copy.43 = bf16[2,768,2048]{2,1,0:T(8,128)(2,1)} copy(bf16[2,768,2048]{2,0,1:T(2,128)(2,1)} %all-to-all-done.1) | data formatting | bytes 12582912 | tf_op jit(solution)/shard_map/all_to_all | solution.py:79
  558.5 14.4 %gather_fusion.3 = bf16[1280,2048]{1,0:T(8,128)(2,1)} fusion(bf16[1536,2048]{1,0:T(8,128)(2,1)} %bitcast.12, s32[2048]{0:T(1024)S(1)} %pad_clamp_fusion), kind=kCustom, calls=%fused_computation.3 | custom fusion | bytes 10490880 | tf_op jit(solution)/shard_map/gather | solution.py:61
  572.9 10.4 %reshape.158 = f32[128,10,2048]{2,1,0:T(8,128)} reshape(bf16[1280,2048]{1,0:T(8,128)(2,1)} %gather_fusion.3) | data formatting | bytes 15728640 | tf_op jit(solution)/shard_map/convert_element_type | solution.py:62
  583.3 99.6 %all-to-all-done.3 = bf16[2,768,2048]{2,0,1:T(2,128)(2,1)} async-done(((bf16[2,768,2048]{2,0,1:T(2,128)(2,1)}), bf16[2,768,2048]{2,0,1:T(2,128)(2,1)}, u32[]{:S(2)}, u32[]{:S(2)}) %all-to-all-start.3) | async-done | bytes 6291488 | tf_op jit(solution)/shard_map/all_to_all | solution.py:84
  682.9 8.3 %copy.49 = bf16[2,768,2048]{2,1,0:T(8,128)(2,1)} copy(bf16[2,768,2048]{2,0,1:T(2,128)(2,1)} %all-to-all-done.3) | data formatting | bytes 12582912 | tf_op jit(solution)/shard_map/all_to_all | solution.py:84
  691.2 14.4 %gather_fusion.5 = bf16[1280,2048]{1,0:T(8,128)(2,1)} fusion(bf16[1536,2048]{1,0:T(8,128)(2,1)} %bitcast.11, s32[2048]{0:T(1024)S(1)} %pad_clamp_fusion), kind=kCustom, calls=%fused_computation.5 | custom fusion | bytes 10490880 | tf_op jit(solution)/shard_map/gather | solution.py:61
  705.6 10.4 %reshape.159 = f32[128,10,2048]{2,1,0:T(8,128)} reshape(bf16[1280,2048]{1,0:T(8,128)(2,1)} %gather_fusion.5) | data formatting | bytes 15728640 | tf_op jit(solution)/shard_map/convert_element_type | solution.py:62
  716.0 15.2 %multiply_reduce_fusion = (f32[128,2048]{1,0:T(8,128)}, f32[128,2048]{1,0:T(8,128)}) fusion(f32[128,10,2048]{2,1,0:T(8,128)} %reshape.159, f32[128,10]{1,0:T(8,128)S(1)} %copy.44, f32[128,10,2048]{2,1,0:T(8,128)} %reshape.158), kind=kLoop, calls=%fused_computation.8 | loop fusion | flops 9961472 | bytes 23073792 | tf_op jit(solution)/shard_map/reduce_sum | solution.py:62
  (21 shorter events, 0.2 us)
Async XLA Ops:
  0.6 355.0 %copy-start = (bf16[2,256,2048]{2,1,0:T(8,128)(2,1)S(1)}, bf16[2,256,2048]{2,1,0:T(8,128)(2,1)}, u32[]{:S(2)}) copy-start(bf16[2,256,2048]{2,1,0:T(8,128)(2,1)} %param.13) | copy-start | bytes 6291460
  14.8 13.3 %copy-start.2 = (bf16[128,2048]{1,0:T(8,128)(2,1)S(1)}, bf16[128,2048]{1,0:T(8,128)(2,1)}, u32[]{:S(2)}) copy-start(bf16[128,2048]{1,0:T(8,128)(2,1)} %param.7) | copy-start | bytes 1572868
  47.9 15.5 %copy-start.3 = (bf16[128,2048]{1,0:T(8,128)(2,1)S(1)}, bf16[128,2048]{1,0:T(8,128)(2,1)}, u32[]{:S(2)}) copy-start(bf16[128,2048]{1,0:T(8,128)(2,1)} %param.8) | copy-start | bytes 1572868
  47.9 159.0 %all-to-all-start = ((bf16[2,768,2048]{2,0,1:T(2,128)(2,1)}), bf16[2,768,2048]{2,0,1:T(2,128)(2,1)}, u32[]{:S(2)}, u32[]{:S(2)}) async-start(bf16[2,768,2048]{2,0,1:T(2,128)(2,1)} %copy.36), calls=%async_computation | async-start | bytes 12582912 | tf_op jit(solution)/shard_map/all_to_all | solution.py:75
  206.9 148.7 %all-to-all-start.2 = ((bf16[2,768,2048]{2,0,1:T(2,128)(2,1)}), bf16[2,768,2048]{2,0,1:T(2,128)(2,1)}, u32[]{:S(2)}, u32[]{:S(2)}) async-start(bf16[2,768,2048]{2,0,1:T(2,128)(2,1)} %copy.45), calls=%async_computation.2 | async-start | bytes 12582912 | tf_op jit(solution)/shard_map/all_to_all | solution.py:80
  355.6 7.2 copy-start.6
  355.6 7.2 copy-start.7
  390.7 7.0 copy-start.5
  390.7 146.6 %all-to-all-start.1 = ((bf16[2,768,2048]{2,0,1:T(2,128)(2,1)}), bf16[2,768,2048]{2,0,1:T(2,128)(2,1)}, u32[]{:S(2)}, u32[]{:S(2)}) async-start(bf16[2,768,2048]{2,0,1:T(2,128)(2,1)} %copy.42), calls=%async_computation.1 | async-start | bytes 12582912 | tf_op jit(solution)/shard_map/all_to_all | solution.py:79
  422.0 128.0 %copy-start.4 = (f32[128,10]{0,1:T(8,128)S(1)}, f32[128,10]{0,1:T(8,128)}, u32[]{:S(2)}) copy-start(f32[128,10]{0,1:T(8,128)} %param.10) | copy-start | bytes 15364
  537.3 145.6 %all-to-all-start.3 = ((bf16[2,768,2048]{2,0,1:T(2,128)(2,1)}), bf16[2,768,2048]{2,0,1:T(2,128)(2,1)}, u32[]{:S(2)}, u32[]{:S(2)}) async-start(bf16[2,768,2048]{2,0,1:T(2,128)(2,1)} %copy.48), calls=%async_computation.3 | async-start | bytes 12582912 | tf_op jit(solution)/shard_map/all_to_all | solution.py:84
  716.0 15.2 %copy-start.1 = (bf16[2,256,2048]{2,1,0:T(8,128)(2,1)S(1)}, bf16[2,256,2048]{2,1,0:T(8,128)(2,1)}, u32[]{:S(2)}) copy-start(bf16[2,256,2048]{2,1,0:T(8,128)(2,1)} %param.13) | copy-start | bytes 6291460
where the time goes:
time: 740 us; the launch traced here: 731 us
  waiting for transfers between devices  472 us (64%)
  local copies, waits for them, and re-layouts  171 us (23%)
  starting transfers between devices  37.9 us (5%)
  matrix products  28.4 us (4%)
  other arithmetic  21.1 us (3%)
    all_to_all x1, waiting for transfers between devices, on_device(): lax.all_to_all(send_grads, 'expert', split_axis=1, concat_axis=1, tiled=T...  134 us
    all_to_all x1, waiting for transfers between devices, on_device(): lax.all_to_all(send_rows, 'expert', split_axis=1, concat_axis=1, tiled=True)  124 us
    all_to_all x1, waiting for transfers between devices, on_device(): lax.all_to_all(expert_out, 'expert', split_axis=1, concat_axis=1, tiled=T...  115 us
    all_to_all x1, waiting for transfers between devices, on_device(): lax.all_to_all(expert_back, 'expert', split_axis=1, concat_axis=1, tiled=...  99.6 us
    gather x2, local copies, waits for them, and re-layouts, combine_rows(): flat_back[target_of].reshape(token_count, top_count, returned.shape[2])  28.8 us
    reshape x2, local copies, waits for them, and re-layouts, pack_rows(): return picked.reshape(local_count, -1, values.shape[1])  25.3 us
    convert_element_type x2, local copies, waits for them, and re-layouts, combine_rows(): return jnp.sum(picked.astype(jnp.float32) * probs[:, :, None], axis=1)  20.8 us
    convert_element_type x1, local copies, waits for them, and re-layouts, forward_part(): return (expert_out.astype(jnp.bfloat16), gate_pre, up_pre, sigmoid_gate)  19.2 us
  transfers between devices with their start and end apart: 4, of which 4 were waited for; matrix products, arithmetic and copies ran while one was open for 12% of the time, Pallas kernels for 0%

commit v1 on v0

v1 whole, which is shorter than its diff:
```python
import functools

import jax
import jax.numpy as jnp
from jax import lax
from jax.experimental import pallas as pl
from jax.experimental.pallas import tpu as pltpu
from jax.sharding import PartitionSpec as P

MESH = pl.DeviceIdType.MESH
F32 = jnp.float32
BF16 = jnp.bfloat16
NT = (((1,), (1,)), ((), ()))

PY, PX, Z = 4, 4, 8
CAP = 6
CHUNK = 256


def moe_kernel(
    cfg, meta, tok, cot, wg_hbm, wu_hbm, wd_hbm, o_mix, o_grad,
    gat, stg, rcv, wg, wu, wd, pm, wt, wtmp, gu, ga, act, gg, pt, sb, mt,
    l_sem, w_sem, m_send, m_recv, zg_send, zg_recv, d_send, d_recv, d_self,
    r_send, r_recv, r_self, zr_send, zr_recv, credit,
):
    py, px, nz, cap, tk, top, dim, hid, el, cw = cfg
    nc = dim // cw
    nch = 2 * nc
    cols = py * px
    sl = nz * cap
    blk = el * sl
    nm = nz // 2
    np_ = nz - 1 - nm
    me = lax.axis_index("expert")
    z = lax.rem(me, nz)
    col = me // nz
    x = lax.rem(col, px)
    y = col // px

    def peer(c, zz):
        return {"expert": c * nz + zz}

    zup = lax.rem(z + 1, nz)
    zdn = lax.rem(z + nz - 1, nz)

    def colat(oy, ox):
        return lax.rem(y + oy, py) * px + lax.rem(x + ox, px)

    def own(ch, src, off):
        return pltpu.make_async_copy(
            src.at[:, pl.ds(pl.multiple_of(off * cw, cw), cw)], gat.at[ch, z], l_sem.at[ch]
        )

    for c in range(nc):
        own(c, tok, c).start()
    w_copies = [
        pltpu.make_async_copy(wg_hbm, wg, w_sem.at[0]),
        pltpu.make_async_copy(wu_hbm, wu, w_sem.at[1]),
        pltpu.make_async_copy(wd_hbm, wd, w_sem.at[2]),
    ]

    bar = pltpu.get_barrier_semaphore()

    def sig_plane(i, _):
        pl.semaphore_signal(
            bar, inc=1, device_id=peer(lax.rem(col + i, cols), z), device_id_type=MESH
        )
        return 0

    def sig_line(i, _):
        pl.semaphore_signal(
            bar, inc=1, device_id=peer(col, lax.rem(z + i, nz)), device_id_type=MESH
        )
        return 0

    lax.fori_loop(1, cols, sig_plane, 0)
    lax.fori_loop(1, nz, sig_line, 0)
    pl.semaphore_wait(bar, cols + nz - 2)

    def send_meta(i, _):
        pltpu.make_async_remote_copy(
            src_ref=meta, dst_ref=mt.at[z], send_sem=m_send.at[i - 1],
            recv_sem=m_recv.at[i - 1], device_id=peer(col, lax.rem(z + i, nz)),
            device_id_type=MESH,
        ).start()
        return 0

    lax.fori_loop(1, nz, send_meta, 0)

    def ring(ch, s):
        b = lax.rem(z - s + 1 + nz, nz)
        pltpu.make_async_remote_copy(
            src_ref=gat.at[ch, b], dst_ref=gat.at[ch, b], send_sem=zg_send.at[ch],
            recv_sem=zg_recv.at[ch, s - 1], device_id=peer(col, zup), device_id_type=MESH,
        ).start()
        if s <= np_:
            b = lax.rem(z + s - 1, nz)
            pltpu.make_async_remote_copy(
                src_ref=gat.at[ch, b], dst_ref=gat.at[ch, b], send_sem=zg_send.at[ch],
                recv_sem=zg_recv.at[ch, nm + s - 1], device_id=peer(col, zdn),
                device_id_type=MESH,
            ).start()

    def ring_wait(ch, s):
        b = lax.rem(z - s + nz, nz)
        pltpu.make_async_copy(gat.at[ch, b], gat.at[ch, b], zg_recv.at[ch, s - 1]).wait()
        if s <= np_:
            b = lax.rem(z + s, nz)
            pltpu.make_async_copy(
                gat.at[ch, b], gat.at[ch, b], zg_recv.at[ch, nm + s - 1]
            ).wait()

    def ring_first(ch):
        pltpu.make_async_copy(gat.at[ch, z], gat.at[ch, z], l_sem.at[ch]).wait()
        ring(ch, 1)

    def ring_event(ch, s):
        ring_wait(ch, s)
        if s < nm:
            ring(ch, s + 1)

    ring_first(0)
    ring_first(1)
    for c in range(nc):
        own(nc + c, cot, c).start()
    for w in w_copies:
        w.start()

    mt[z] = meta[...]

    def wait_meta(i, _):
        pltpu.make_async_copy(mt.at[z], mt.at[z], m_recv.at[i - 1]).wait()
        return 0

    lax.fori_loop(1, nz, wait_meta, 0)
    exs = cols * el
    before = (
        lax.broadcasted_iota(jnp.int32, (tk, tk), 0) < lax.broadcasted_iota(jnp.int32, (tk, tk), 1)
    ).astype(F32).astype(BF16)
    eye = (
        lax.broadcasted_iota(jnp.int32, (tk, tk), 0) == lax.broadcasted_iota(jnp.int32, (tk, tk), 1)
    ).astype(F32).astype(BF16)
    half = mt.shape[1] // 2

    def route(b, cnt):
        ids = mt[b, 0:half, :].astype(jnp.int32)
        pr = mt[b, half : 2 * half, :]
        lab = lax.broadcasted_iota(jnp.int32, (exs, tk), 0)
        member = jnp.zeros((exs, tk), F32)
        weight = jnp.zeros((exs, tk), F32)
        for k in range(top):
            idk = ids[k : k + 1, :]
            code = (idk // (el * nz)) * el + lax.rem(idk, el)
            code = jnp.where(lax.rem(idk // el, nz) == z, code, -1)
            hit = lab == code
            member = jnp.where(hit, 1.0, member)
            weight = jnp.where(hit, pr[k : k + 1, :], weight)
        rank = jnp.dot(member.astype(BF16), before, preferred_element_type=F32) + cnt
        rank = jnp.where(member > 0.5, rank, -1.0).astype(jnp.int32)
        hi = weight.astype(BF16).astype(F32)
        lo = weight - hi
        at = pl.ds(pl.multiple_of(b * tk, tk), tk)
        for ex in range(exs):
            j = lax.broadcasted_iota(jnp.int32, (sl, tk), 0)
            hit = j == rank[ex : ex + 1, :]
            rows = pl.ds(ex * sl, sl)
            pm[rows, at] = jnp.where(hit, 1.0, 0.0).astype(BF16)
            wtmp[0, rows, :] = jnp.where(hit, hi[ex : ex + 1, :], 0.0).astype(BF16)
            wtmp[1, rows, :] = jnp.where(hit, lo[ex : ex + 1, :], 0.0).astype(BF16)
        for i in range(2):
            wt[i, at, :] = lax.dot_general(
                eye, wtmp[i], NT, preferred_element_type=F32
            ).astype(BF16)
        return cnt + jnp.sum(member, axis=1, keepdims=True)

    lax.fori_loop(0, nz, route, jnp.zeros((exs, 1), F32))

    def ring_guarded(ch, s):
        @pl.when(ch < nch)
        def _():
            ring_event(ch, s)

    h1 = nm // 2
    for s in range(1, nm + 1):
        ring_event(0, s)
        if s <= h1:
            ring_event(1, s)
    ring_first(2)
    events = []
    for i in range(max(h1, nm - h1)):
        if h1 + 1 + i <= nm:
            events.append((1, h1 + 1 + i))
        if i < h1:
            events.append((2, 1 + i))
    for w in w_copies:
        w.wait()

    def acc_part(ch, q):
        ys = lax.rem(y - q + py, py)
        rows = pl.ds(ys * px, px)

        @pl.when(q == 0)
        def _():
            pltpu.make_async_copy(rcv.at[ch, col], rcv.at[ch, col], d_self.at[ch]).wait()
            pltpu.make_async_copy(
                rcv.at[ch, pl.ds(0, px - 1)], rcv.at[ch, pl.ds(0, px - 1)], d_recv.at[ch, q]
            ).wait()

        @pl.when(q > 0)
        def _():
            pltpu.make_async_copy(
                rcv.at[ch, pl.ds(0, px)], rcv.at[ch, pl.ds(0, px)], d_recv.at[ch, q]
            ).wait()

        def block(e):
            return rcv[ch, rows, pl.ds(e * sl, sl), :].reshape(px * sl, cw)

        @pl.when(ch < nc)
        def _():
            at = pl.ds(pl.multiple_of(ch * cw, cw), cw)
            for e in range(el):
                v = block(e)
                for h, w in ((0, wg), (1, wu)):
                    r = jnp.dot(v, w[e, at, :], preferred_element_type=F32)
                    gu[h, e, rows] += r.reshape(px, sl, hid)

        @pl.when(ch >= nc)
        def _():
            at = pl.ds(pl.multiple_of((ch - nc) * cw, cw), cw)
            for e in range(el):
                r = lax.dot_general(block(e), wd[e, :, at], NT, preferred_element_type=F32)
                ga[e, rows] += r.reshape(px, sl, hid)

    def wait_d_send(ch):
        pltpu.make_async_copy(
            stg.at[ch, pl.ds(0, cols - 1)], stg.at[ch, pl.ds(0, cols - 1)], d_send.at[ch]
        ).wait()

    gu[...] = jnp.zeros_like(gu)
    ga[...] = jnp.zeros_like(ga)

    def dispatch(i, _):
        ch = i // py
        q = lax.rem(i, py)
        for k, (d, s) in enumerate(events):
            @pl.when(q == k * py // len(events))
            def _():
                ring_guarded(ch + d, s)

        @pl.when((q == py - 1) & (ch + 3 < nch))
        def _():
            ring_first(ch + 3)

        @pl.when((q == 0) & (ch >= 2))
        def _():
            wait_d_send(ch - 2)

        yd = lax.rem(y + q, py)
        rows = pl.ds(pl.multiple_of(yd * (px * blk), px * blk), px * blk)
        packed = jnp.dot(
            pm[rows, :], gat[ch].reshape(nz * tk, cw), preferred_element_type=F32
        )
        stg[ch, pl.ds(yd * px, px)] = packed.astype(BF16).reshape(px, blk, cw)

        @pl.when(ch >= 2)
        def _():
            acc_part(ch - 2, q)

        for ox in range(px):
            d = colat(q, ox)

            def remote():
                pltpu.make_async_remote_copy(
                    src_ref=stg.at[ch, d], dst_ref=rcv.at[ch, col], send_sem=d_send.at[ch],
                    recv_sem=d_recv.at[ch, q], device_id=peer(d, z), device_id_type=MESH,
                ).start()

            if ox == 0:
                @pl.when(q == 0)
                def _():
                    pltpu.make_async_copy(
                        stg.at[ch, col], rcv.at[ch, col], d_self.at[ch]
                    ).start()

                @pl.when(q > 0)
                def _():
                    remote()
            else:
                remote()
        return 0

    lax.fori_loop(0, nch * py, dispatch, 0)

    def wait_zg(ch, _):
        pltpu.make_async_copy(
            gat.at[ch, pl.ds(0, nz - 1)], gat.at[ch, pl.ds(0, nz - 1)], zg_send.at[ch]
        ).wait()
        return 0

    lax.fori_loop(0, nch, wait_zg, 0)
    for zz in (zup, zdn):
        pl.semaphore_signal(credit, inc=1, device_id=peer(col, zz), device_id_type=MESH)

    def forward_act(p, _):
        for e in range(el):
            g = gu[0, e, p]
            act[e, p] = (g * jax.nn.sigmoid(g) * gu[1, e, p]).astype(BF16)
        return 0

    lax.fori_loop(0, cols, forward_act, 0)

    def backward_act(p, _):
        for e in range(el):
            g = gu[0, e, p]
            sig = jax.nn.sigmoid(g)
            d = ga[e, p]
            gg[0, e, p] = (d * gu[1, e, p] * sig * (1.0 + g * (1.0 - sig))).astype(BF16)
            gg[1, e, p] = (d * g * sig).astype(BF16)
        return 0

    def expert_part(r, q):
        rows = pl.ds(lax.rem(y + q, py) * px, px)

        @pl.when(r < nc)
        def _():
            at = pl.ds(pl.multiple_of(r * cw, cw), cw)
            for e in range(el):
                v = act[e, rows].reshape(px * sl, hid)
                o = jnp.dot(v, wd[e, :, at], preferred_element_type=F32)
                rcv[r, rows, pl.ds(e * sl, sl), :] = o.astype(BF16).reshape(px, sl, cw)

        @pl.when(r >= nc)
        def _():
            at = pl.ds(pl.multiple_of((r - nc) * cw, cw), cw)
            for e in range(el):
                o = lax.dot_general(
                    gg[0, e, rows].reshape(px * sl, hid), wg[e, at, :], NT,
                    preferred_element_type=F32,
                ) + lax.dot_general(
                    gg[1, e, rows].reshape(px * sl, hid), wu[e, at, :], NT,
                    preferred_element_type=F32,
                )
                rcv[r, rows, pl.ds(e * sl, sl), :] = o.astype(BF16).reshape(px, sl, cw)

    bq = nz // py

    def combine_part(c, q):
        @pl.when(q == 0)
        def _():
            pltpu.make_async_copy(stg.at[c, col], stg.at[c, col], r_self.at[c]).wait()
            for k in range(py):
                n = px - 1 if k == 0 else px
                pltpu.make_async_copy(
                    stg.at[c, pl.ds(0, n)], stg.at[c, pl.ds(0, n)], r_recv.at[c, k]
                ).wait()

        rows = pl.ds(pl.multiple_of(q * (bq * tk), bq * tk), bq * tk)
        v = stg[c].reshape(cols * blk, cw)
        o = jnp.dot(wt[0, rows, :], v, preferred_element_type=F32) + jnp.dot(
            wt[1, rows, :], v, preferred_element_type=F32
        )
        pt[lax.rem(c, 3), pl.ds(q * bq, bq)] = o.reshape(bq, tk, cw)

    def sum_send(c, s, dn):
        slot = lax.rem(c, 3)
        i = s - 1 if dn else nm + s - 1
        b = lax.rem(z - nm + s - 1 + nz, nz) if dn else lax.rem(z + np_ + 1 - s, nz)
        v = pt[slot, b]
        if s > 1:
            v = v + gat[c, i - 1].astype(F32)
        sb[slot, i] = v.astype(BF16)
        pltpu.make_async_remote_copy(
            src_ref=sb.at[slot, i], dst_ref=gat.at[c, i], send_sem=zr_send.at[c],
            recv_sem=zr_recv.at[c, i], device_id=peer(col, zdn if dn else zup),
            device_id_type=MESH,
        ).start()

    def sum_wait(c, i):
        pltpu.make_async_copy(gat.at[c, i], gat.at[c, i], zr_recv.at[c, i]).wait()

    def sum_event(c, s):
        if s > 1:
            sum_wait(c, s - 2)
            if s - 1 <= np_:
                sum_wait(c, nm + s - 2)
        if s <= nm:
            sum_send(c, s, True)
        if s <= np_:
            sum_send(c, s, False)
        if s == nm + 1:
            slot = lax.rem(c, 3)
            total = pt[slot, z] + gat[c, nm - 1].astype(F32)
            if np_ > 0:
                total = total + gat[c, nm + np_ - 1].astype(F32)

            @pl.when(c < nc)
            def _():
                o_mix[:, pl.ds(pl.multiple_of(c * cw, cw), cw)] = total

            @pl.when(c >= nc)
            def _():
                o_grad[:, pl.ds(pl.multiple_of((c - nc) * cw, cw), cw)] = total

            pltpu.make_async_copy(
                gat.at[c, pl.ds(0, nz - 1)], gat.at[c, pl.ds(0, nz - 1)], zr_send.at[c]
            ).wait()

    sums = []
    for s in range(1, nm + 2):
        tick = (s - 1) * max(1, 2 * py // nm // 1) if nm < 4 else (s - 1) * 2
        tick = min(tick, 2 * py)
        sums.append((3 + tick // py, tick % py, s))
    last = nch + max(d for d, _, _ in sums)

    def give_back(i, _):
        r = i // py
        q = lax.rem(i, py)

        @pl.when((r == 3) & (q == 0))
        def _():
            pl.semaphore_wait(credit, 2)

        for d, k, s in sorted(sums, key=lambda v: (-v[0], v[1])):
            @pl.when((q == k) & (r >= d) & (r - d < nch))
            def _():
                sum_event(r - d, s)

        @pl.when((q == 0) & (r < 2))
        def _():
            wait_d_send(nch - 2 + r)

        @pl.when(r < nch)
        def _():
            expert_part(r, q)

        @pl.when(r < 2)
        def _():
            acc_part(nch - 2 + r, q)

            @pl.when((r == 1) & (q == py - 1))
            def _():
                lax.fori_loop(0, cols, backward_act, 0)

        @pl.when((r >= 2) & (r - 2 < nch))
        def _():
            combine_part(r - 2, q)

        @pl.when(r < nch)
        def _():
            for ox in range(px):
                d = colat(q, ox)

                def remote():
                    pltpu.make_async_remote_copy(
                        src_ref=rcv.at[r, d], dst_ref=stg.at[r, col], send_sem=r_send.at[r],
                        recv_sem=r_recv.at[r, q], device_id=peer(d, z), device_id_type=MESH,
                    ).start()

                if ox == 0:
                    @pl.when(q == 0)
                    def _():
                        pltpu.make_async_copy(
                            rcv.at[r, col], stg.at[r, col], r_self.at[r]
                        ).start()

                    @pl.when(q > 0)
                    def _():
                        remote()
                else:
                    remote()

        return 0

    lax.fori_loop(0, last * py, give_back, 0)

    def finish(ch, _):
        pltpu.make_async_copy(
            rcv.at[ch, pl.ds(0, cols - 1)], rcv.at[ch, pl.ds(0, cols - 1)], r_send.at[ch]
        ).wait()
        return 0

    lax.fori_loop(0, nch, finish, 0)

    def finish_meta(i, _):
        pltpu.make_async_copy(mt.at[z], mt.at[z], m_send.at[i - 1]).wait()
        return 0

    lax.fori_loop(1, nz, finish_meta, 0)


def on_device(cfg, tokens, cotangent, expert_ids, probs, gate_weight, up_weight, down_weight):
    py, px, nz, cap, tk, top, dim, hid, el, cw = cfg
    nch = 2 * (dim // cw)
    cols = py * px
    sl = nz * cap
    blk = el * sl
    half = -(-top // 8) * 8
    pad = ((0, half - top), (0, 0))
    meta = jnp.concatenate(
        [jnp.pad(expert_ids.T.astype(F32), pad), jnp.pad(probs.T, pad)], axis=0
    )
    vm = pl.BlockSpec(memory_space=pltpu.VMEM)
    hbm = pl.BlockSpec(memory_space=pl.ANY)
    dma = pltpu.SemaphoreType.DMA
    return pl.pallas_call(
        functools.partial(moe_kernel, cfg),
        out_shape=(
            jax.ShapeDtypeStruct((tk, dim), F32),
            jax.ShapeDtypeStruct((tk, dim), F32),
        ),
        in_specs=[vm, hbm, hbm, hbm, hbm, hbm],
        out_specs=(vm, vm),
        scratch_shapes=[
            pltpu.VMEM((nch, nz, tk, cw), BF16),
            pltpu.VMEM((nch, cols, blk, cw), BF16),
            pltpu.VMEM((nch, cols, blk, cw), BF16),
            pltpu.VMEM(gate_weight.shape, BF16),
            pltpu.VMEM(up_weight.shape, BF16),
            pltpu.VMEM(down_weight.shape, BF16),
            pltpu.VMEM((cols * blk, nz * tk), BF16),
            pltpu.VMEM((2, nz * tk, cols * blk), BF16),
            pltpu.VMEM((2, cols * blk, tk), BF16),
            pltpu.VMEM((2, el, cols, sl, hid), F32),
            pltpu.VMEM((el, cols, sl, hid), F32),
            pltpu.VMEM((el, cols, sl, hid), BF16),
            pltpu.VMEM((2, el, cols, sl, hid), BF16),
            pltpu.VMEM((3, nz, tk, cw), F32),
            pltpu.VMEM((3, nz - 1, tk, cw), BF16),
            pltpu.VMEM((nz, 2 * half, tk), F32),
            dma((nch,)),
            dma((3,)),
            dma((nz - 1,)),
            dma((nz - 1,)),
            dma((nch,)),
            dma((nch, nz - 1)),
            dma((nch,)),
            dma((nch, py)),
            dma((nch,)),
            dma((nch,)),
            dma((nch, py)),
            dma((nch,)),
            dma((nch,)),
            dma((nch, nz - 1)),
            pltpu.SemaphoreType.REGULAR,
        ],
        compiler_params=pltpu.CompilerParams(
            collective_id=0, has_side_effects=True, vmem_limit_bytes=67043328
        ),
        name="moe",
    )(meta, tokens, cotangent, gate_weight, up_weight, down_weight)


def solution(mesh):
    rows = P(("dp", "expert"), None)
    cubes = P(("dp", "expert"), None, None)

    def body(tokens, cotangent, expert_ids, probs, gate_weight, up_weight, down_weight):
        tk, dim = tokens.shape
        cfg = (PY, PX, Z, CAP, tk, expert_ids.shape[1], dim, gate_weight.shape[2],
               gate_weight.shape[0], min(CHUNK, dim // 2))
        return on_device(
            cfg, tokens, cotangent, expert_ids, probs, gate_weight, up_weight, down_weight
        )

    return jax.shard_map(
        body, mesh=mesh, in_specs=(rows,) * 4 + (cubes,) * 3, out_specs=(rows, rows),
        check_vma=False,
    )
```

time: 740 us -> 384 us (0.52); the launches traced: 731 us -> 383 us
  waiting for transfers between devices: 472 us -> 0 us
  Pallas kernels: 0 us -> 377 us
  local copies, waits for them, and re-layouts: 171 us -> 3.36 us
  starting transfers between devices: 37.9 us -> 0 us
  matrix products: 28.4 us -> 0 us
  other arithmetic: 21.1 us -> 2.01 us
    all_to_all x4 -> x0, waiting for transfers between devices: 472 us -> none  [the longest x1 134 us: on_device(): lax.all_to_all(send_grads, 'expert', split_axis=1, concat_axis=1, tiled=T...]
    pallas_call x0 -> x1, Pallas kernels: none -> 377 us  [on_device(): pl.pallas_call(functools.partial(moe_kernel, cfg), out_shape=(jax.ShapeDt...]
    convert_element_type x4 -> x0, local copies, waits for them, and re-layouts: 58.7 us -> none  [the longest x2 20.8 us: combine_rows(): return jnp.sum(picked.astype(jnp.float32) * probs[:, :, None], axis=1)]
    gather x6 -> x0, local copies, waits for them, and re-layouts: 58 us -> none  [the longest x2 28.8 us: combine_rows(): flat_back[target_of].reshape(token_count, top_count, returned.shape[2])]
    all_to_all x4 -> x0, starting transfers between devices: 37.9 us -> none  [the longest x1 15.5 us: on_device(): lax.all_to_all(send_rows, 'expert', split_axis=1, concat_axis=1, tiled=True)]
    dot_general x5 -> x0, matrix products: 28.4 us -> none  [the longest x1 7.2 us: backward_part(): jnp.einsum('erd,ehd->erh', grad_rows, down_weight, preferred_element_type...]
    reshape x3 -> x0, local copies, waits for them, and re-layouts: 25.4 us -> none  [the longest x2 25.3 us: pack_rows(): return picked.reshape(local_count, -1, values.shape[1])]
    all_to_all x2 -> x0, local copies, waits for them, and re-layouts: 16.7 us -> none  [the longest x1 8.34 us: on_device(): lax.all_to_all(expert_out, 'expert', split_axis=1, concat_axis=1, tiled=T...]
  transfers between devices with their start and end apart: 4 -> 0, of which waited for: 4 -> 0; matrix products, arithmetic and copies ran while one was open for 12% -> 0% of each run, Pallas kernels for 0% -> 0%
where the time goes in v1:
time: 384 us; the launch traced here: 383 us
  Pallas kernels  377 us (98%)
    pallas_call x1, Pallas kernels, on_device(): pl.pallas_call(functools.partial(moe_kernel, cfg), out_shape=(jax.ShapeDt...  377 us

profile of v1, /device:TPU:32, one launch (start us, length us, event | category | flops | bytes accessed | tf_op | source)
XLA Modules:
  0.0 383.2 jit_solution(13503507679335043182)
XLA Ops:
  0.6 0.7 convert_bitcast_fusion
  1.3 1.3 select_maximum_fusion.meta
  2.6 377.2 %moe.1 = (f32[128,2048]{1,0:T(8,128)}, f32[128,2048]{1,0:T(8,128)}) custom-call(f32[32,128]{1,0:T(8,128)} %select_maximum_fusion.meta, bf16[128,2048]{1,0:T(8,128)(2,1)} %tok.1, bf16[128,2048]{1,0:T(8,128)(2,1)} %cot.1, bf16[2,2048,256]{2,1,0:T(8,128)(2,1)} %wg_hbm.1, bf16[2,2048,256]{2,1,0:T(8,128)(2,1)} %wu_hbm.1, bf16[2,256,2048]{2,1,0:T(8,128)(2,1)} %wd_hbm.1), custom_call_target="tpu_custom_call" | custom-call | tf_op jit(solution)/shard_map/moe/pallas_call | solution.py:505
  379.9 0.0 copy-start
  379.9 2.4 copy.11
  382.3 0.0 copy-done
  382.3 1.0 copy.12
Async XLA Ops:
  379.9 2.4 copy-start

commit v2 on v1

--- a/solution.py
+++ b/solution.py
@@ -15,13 +15,14 @@
 PY, PX, Z = 4, 4, 8
 CAP = 6
 CHUNK = 256
+STRIDE = 3
 
 
 def moe_kernel(
     cfg, meta, tok, cot, wg_hbm, wu_hbm, wd_hbm, o_mix, o_grad,
-    gat, stg, rcv, wg, wu, wd, pm, wt, wtmp, gu, ga, act, gg, pt, sb, mt,
+    gat, stg, rcv, wg, wu, wd, pm, wt, gu, ga, act, gg, pt, sb, ost, mt,
     l_sem, w_sem, m_send, m_recv, zg_send, zg_recv, d_send, d_recv, d_self,
-    r_send, r_recv, r_self, zr_send, zr_recv, credit,
+    r_send, r_recv, r_self, zr_send, zr_recv, o_sem, credit,
 ):
     py, px, nz, cap, tk, top, dim, hid, el, cw = cfg
     nc = dim // cw
@@ -31,6 +32,7 @@
     blk = el * sl
     nm = nz // 2
     np_ = nz - 1 - nm
+    slots = pt.shape[0]
     me = lax.axis_index("expert")
     z = lax.rem(me, nz)
     col = me // nz
@@ -40,8 +42,13 @@
     def peer(c, zz):
         return {"expert": c * nz + zz}
 
-    zup = lax.rem(z + 1, nz)
-    zdn = lax.rem(z + nz - 1, nz)
+    sense = 1 - 2 * lax.rem(lax.axis_index("dp"), 2)
+
+    def along(n):
+        return lax.rem(z + sense * n + 2 * nz, nz)
+
+    zup = along(1)
+    zdn = along(-1)
 
     def colat(oy, ox):
         return lax.rem(y + oy, py) * px + lax.rem(x + ox, px)
@@ -88,13 +95,13 @@
     lax.fori_loop(1, nz, send_meta, 0)
 
     def ring(ch, s):
-        b = lax.rem(z - s + 1 + nz, nz)
+        b = along(1 - s)
         pltpu.make_async_remote_copy(
             src_ref=gat.at[ch, b], dst_ref=gat.at[ch, b], send_sem=zg_send.at[ch],
             recv_sem=zg_recv.at[ch, s - 1], device_id=peer(col, zup), device_id_type=MESH,
         ).start()
         if s <= np_:
-            b = lax.rem(z + s - 1, nz)
+            b = along(s - 1)
             pltpu.make_async_remote_copy(
                 src_ref=gat.at[ch, b], dst_ref=gat.at[ch, b], send_sem=zg_send.at[ch],
                 recv_sem=zg_recv.at[ch, nm + s - 1], device_id=peer(col, zdn),
@@ -102,10 +109,10 @@
             ).start()
 
     def ring_wait(ch, s):
-        b = lax.rem(z - s + nz, nz)
+        b = along(-s)
         pltpu.make_async_copy(gat.at[ch, b], gat.at[ch, b], zg_recv.at[ch, s - 1]).wait()
         if s <= np_:
-            b = lax.rem(z + s, nz)
+            b = along(s)
             pltpu.make_async_copy(
                 gat.at[ch, b], gat.at[ch, b], zg_recv.at[ch, nm + s - 1]
             ).wait()
@@ -119,8 +126,20 @@
         if s < nm:
             ring(ch, s + 1)
 
-    ring_first(0)
-    ring_first(1)
+    steps = [(-1 - STRIDE * (nm - s), s) for s in range(nm + 1)]
+    early = sorted(
+        (t + py * ch, ch, s) for t, s in steps for ch in range(nch) if t + py * ch < 0
+    )
+    steps = sorted((t % py, -(t // py), s) for t, s in steps)
+
+    def step(ch, s):
+        if s == 0:
+            ring_first(ch)
+        else:
+            ring_event(ch, s)
+
+    step(*early[0][1:])
+    early = early[1:]
     for c in range(nc):
         own(nc + c, cot, c).start()
     for w in w_copies:
@@ -165,33 +184,25 @@
             hit = j == rank[ex : ex + 1, :]
             rows = pl.ds(ex * sl, sl)
             pm[rows, at] = jnp.where(hit, 1.0, 0.0).astype(BF16)
-            wtmp[0, rows, :] = jnp.where(hit, hi[ex : ex + 1, :], 0.0).astype(BF16)
-            wtmp[1, rows, :] = jnp.where(hit, lo[ex : ex + 1, :], 0.0).astype(BF16)
+            for i, w in enumerate((hi, lo)):
+                stg[nch - 1, ex // el, pl.ds((ex % el) * sl, sl), pl.ds(i * tk, tk)] = (
+                    jnp.where(hit, w[ex : ex + 1, :], 0.0).astype(BF16)
+                )
         for i in range(2):
             wt[i, at, :] = lax.dot_general(
-                eye, wtmp[i], NT, preferred_element_type=F32
+                eye, stg[nch - 1, :, :, pl.ds(i * tk, tk)].reshape(cols * blk, tk), NT,
+                preferred_element_type=F32,
             ).astype(BF16)
         return cnt + jnp.sum(member, axis=1, keepdims=True)
 
-    lax.fori_loop(0, nz, route, jnp.zeros((exs, 1), F32))
-
-    def ring_guarded(ch, s):
-        @pl.when(ch < nch)
-        def _():
-            ring_event(ch, s)
-
-    h1 = nm // 2
-    for s in range(1, nm + 1):
-        ring_event(0, s)
-        if s <= h1:
-            ring_event(1, s)
-    ring_first(2)
-    events = []
-    for i in range(max(h1, nm - h1)):
-        if h1 + 1 + i <= nm:
-            events.append((1, h1 + 1 + i))
-        if i < h1:
-            events.append((2, 1 + i))
+    def route_step(b, cnt):
+        for n, (_, ch, s) in enumerate(early):
+            @pl.when(b == (n * nz) // len(early))
+            def _():
+                step(ch, s)
+        return route(b, cnt)
+
+    lax.fori_loop(0, nz, route_step, jnp.zeros((exs, 1), F32))
     for w in w_copies:
         w.wait()
 
@@ -242,14 +253,10 @@
     def dispatch(i, _):
         ch = i // py
         q = lax.rem(i, py)
-        for k, (d, s) in enumerate(events):
-            @pl.when(q == k * py // len(events))
-            def _():
-                ring_guarded(ch + d, s)
-
-        @pl.when((q == py - 1) & (ch + 3 < nch))
-        def _():
-            ring_first(ch + 3)
+        for k, d, s in steps:
+            @pl.when((q == k) & (ch + d < nch))
+            def _():
+                step(ch + d, s)
 
         @pl.when((q == 0) & (ch >= 2))
         def _():
@@ -359,12 +366,12 @@
         o = jnp.dot(wt[0, rows, :], v, preferred_element_type=F32) + jnp.dot(
             wt[1, rows, :], v, preferred_element_type=F32
         )
-        pt[lax.rem(c, 3), pl.ds(q * bq, bq)] = o.reshape(bq, tk, cw)
+        pt[lax.rem(c, slots), pl.ds(q * bq, bq)] = o.reshape(bq, tk, cw)
 
     def sum_send(c, s, dn):
-        slot = lax.rem(c, 3)
+        slot = lax.rem(c, slots)
         i = s - 1 if dn else nm + s - 1
-        b = lax.rem(z - nm + s - 1 + nz, nz) if dn else lax.rem(z + np_ + 1 - s, nz)
+        b = along(s - 1 - nm) if dn else along(np_ + 1 - s)
         v = pt[slot, b]
         if s > 1:
             v = v + gat[c, i - 1].astype(F32)
@@ -377,6 +384,10 @@
 
     def sum_wait(c, i):
         pltpu.make_async_copy(gat.at[c, i], gat.at[c, i], zr_recv.at[c, i]).wait()
+
+    def out_copy(dst, c, o):
+        at = pl.ds(pl.multiple_of(c * cw, cw), cw)
+        return pltpu.make_async_copy(ost.at[o], dst.at[:, at], o_sem.at[o])
 
     def sum_event(c, s):
         if s > 1:
@@ -388,18 +399,26 @@
         if s <= np_:
             sum_send(c, s, False)
         if s == nm + 1:
-            slot = lax.rem(c, 3)
+            slot = lax.rem(c, slots)
             total = pt[slot, z] + gat[c, nm - 1].astype(F32)
             if np_ > 0:
                 total = total + gat[c, nm + np_ - 1].astype(F32)
 
+            o = lax.rem(c, 2)
+
+            @pl.when(c >= 2)
+            def _():
+                out_copy(o_mix, 0, o).wait()
+
+            ost[o] = total
+
             @pl.when(c < nc)
             def _():
-                o_mix[:, pl.ds(pl.multiple_of(c * cw, cw), cw)] = total
+                out_copy(o_mix, c, o).start()
 
             @pl.when(c >= nc)
             def _():
-                o_grad[:, pl.ds(pl.multiple_of((c - nc) * cw, cw), cw)] = total
+                out_copy(o_grad, c - nc, o).start()
 
             pltpu.make_async_copy(
                 gat.at[c, pl.ds(0, nz - 1)], gat.at[c, pl.ds(0, nz - 1)], zr_send.at[c]
@@ -407,8 +426,7 @@
 
     sums = []
     for s in range(1, nm + 2):
-        tick = (s - 1) * max(1, 2 * py // nm // 1) if nm < 4 else (s - 1) * 2
-        tick = min(tick, 2 * py)
+        tick = STRIDE * (s - 1)
         sums.append((3 + tick // py, tick % py, s))
     last = nch + max(d for d, _, _ in sums)
 
@@ -481,6 +499,9 @@
 
     lax.fori_loop(0, nch, finish, 0)
 
+    for o in range(2):
+        out_copy(o_grad, 0, o).wait()
+
     def finish_meta(i, _):
         pltpu.make_async_copy(mt.at[z], mt.at[z], m_send.at[i - 1]).wait()
         return 0
@@ -494,6 +515,7 @@
     cols = py * px
     sl = nz * cap
     blk = el * sl
+    slots = 1 + -(-(STRIDE * (nz // 2)) // py)
     half = -(-top // 8) * 8
     pad = ((0, half - top), (0, 0))
     meta = jnp.concatenate(
@@ -509,7 +531,7 @@
             jax.ShapeDtypeStruct((tk, dim), F32),
         ),
         in_specs=[vm, hbm, hbm, hbm, hbm, hbm],
-        out_specs=(vm, vm),
+        out_specs=(hbm, hbm),
         scratch_shapes=[
             pltpu.VMEM((nch, nz, tk, cw), BF16),
             pltpu.VMEM((nch, cols, blk, cw), BF16),
@@ -519,13 +541,13 @@
             pltpu.VMEM(down_weight.shape, BF16),
             pltpu.VMEM((cols * blk, nz * tk), BF16),
             pltpu.VMEM((2, nz * tk, cols * blk), BF16),
-            pltpu.VMEM((2, cols * blk, tk), BF16),
             pltpu.VMEM((2, el, cols, sl, hid), F32),
             pltpu.VMEM((el, cols, sl, hid), F32),
             pltpu.VMEM((el, cols, sl, hid), BF16),
             pltpu.VMEM((2, el, cols, sl, hid), BF16),
-            pltpu.VMEM((3, nz, tk, cw), F32),
-            pltpu.VMEM((3, nz - 1, tk, cw), BF16),
+            pltpu.VMEM((slots, nz, tk, cw), F32),
+            pltpu.VMEM((slots, nz - 1, tk, cw), BF16),
+            pltpu.VMEM((2, tk, cw), F32),
             pltpu.VMEM((nz, 2 * half, tk), F32),
             dma((nch,)),
             dma((3,)),
@@ -541,6 +563,7 @@
             dma((nch,)),
             dma((nch,)),
             dma((nch, nz - 1)),
+            dma((2,)),
             pltpu.SemaphoreType.REGULAR,
         ],
         compiler_params=pltpu.CompilerParams(

time: 384 us -> 349 us (0.909)
  Pallas kernels: 377 us -> 341 us
    pallas_call x1, Pallas kernels: 377 us -> 341 us  [on_device(): pl.pallas_call(functools.partial(moe_kernel, cfg), out_shape=(jax.ShapeDt...]
where the time goes in v2:
time: 349 us; the launch traced here: 347 us
  Pallas kernels  341 us (98%)
    pallas_call x1, Pallas kernels, on_device(): pl.pallas_call(functools.partial(moe_kernel, cfg), out_shape=(jax.ShapeDt...  341 us

profile of v2, /device:TPU:32, one launch (start us, length us, event | category | flops | bytes accessed | tf_op | source)
XLA Modules:
  0.0 347.1 jit_solution(3430281189817566900)
XLA Ops:
  0.6 0.7 convert_bitcast_fusion
  1.3 1.3 select_maximum_fusion.meta
  2.6 341.1 %moe.1 = (f32[128,2048]{1,0:T(8,128)}, f32[128,2048]{1,0:T(8,128)}) custom-call(f32[32,128]{1,0:T(8,128)} %select_maximum_fusion.meta, bf16[128,2048]{1,0:T(8,128)(2,1)} %tok.1, bf16[128,2048]{1,0:T(8,128)(2,1)} %cot.1, bf16[2,2048,256]{2,1,0:T(8,128)(2,1)} %wg_hbm.1, bf16[2,2048,256]{2,1,0:T(8,128)(2,1)} %wu_hbm.1, bf16[2,256,2048]{2,1,0:T(8,128)(2,1)} %wd_hbm.1), custom_call_target="tpu_custom_call" | custom-call | tf_op jit(solution)/shard_map/moe/pallas_call | solution.py:527
  343.7 0.0 copy-start
  343.7 2.4 copy.11
  346.1 0.0 copy-done
  346.1 1.0 copy.12
Async XLA Ops:
  343.7 2.4 copy-start

commit v3 on v2

--- a/solution.py
+++ b/solution.py
@@ -16,6 +16,8 @@
 CAP = 6
 CHUNK = 256
 STRIDE = 3
+STRIDE_SUM = 3
+LAG = 4
 
 
 def moe_kernel(
@@ -258,9 +260,9 @@
             def _():
                 step(ch + d, s)
 
-        @pl.when((q == 0) & (ch >= 2))
-        def _():
-            wait_d_send(ch - 2)
+        @pl.when((q == 0) & (ch >= LAG))
+        def _():
+            wait_d_send(ch - LAG)
 
         yd = lax.rem(y + q, py)
         rows = pl.ds(pl.multiple_of(yd * (px * blk), px * blk), px * blk)
@@ -269,9 +271,9 @@
         )
         stg[ch, pl.ds(yd * px, px)] = packed.astype(BF16).reshape(px, blk, cw)
 
-        @pl.when(ch >= 2)
-        def _():
-            acc_part(ch - 2, q)
+        @pl.when(ch >= LAG)
+        def _():
+            acc_part(ch - LAG, q)
 
         for ox in range(px):
             d = colat(q, ox)
@@ -349,24 +351,36 @@
                 )
                 rcv[r, rows, pl.ds(e * sl, sl), :] = o.astype(BF16).reshape(px, sl, cw)
 
-    bq = nz // py
-
     def combine_part(c, q):
         @pl.when(q == 0)
         def _():
             pltpu.make_async_copy(stg.at[c, col], stg.at[c, col], r_self.at[c]).wait()
-            for k in range(py):
-                n = px - 1 if k == 0 else px
-                pltpu.make_async_copy(
-                    stg.at[c, pl.ds(0, n)], stg.at[c, pl.ds(0, n)], r_recv.at[c, k]
-                ).wait()
-
-        rows = pl.ds(pl.multiple_of(q * (bq * tk), bq * tk), bq * tk)
-        v = stg[c].reshape(cols * blk, cw)
-        o = jnp.dot(wt[0, rows, :], v, preferred_element_type=F32) + jnp.dot(
-            wt[1, rows, :], v, preferred_element_type=F32
+            pltpu.make_async_copy(
+                stg.at[c, pl.ds(0, px - 1)], stg.at[c, pl.ds(0, px - 1)], r_recv.at[c, q]
+            ).wait()
+
+        @pl.when(q > 0)
+        def _():
+            pltpu.make_async_copy(
+                stg.at[c, pl.ds(0, px)], stg.at[c, pl.ds(0, px)], r_recv.at[c, q]
+            ).wait()
+
+        ys = lax.rem(y - q + py, py)
+        at = pl.ds(pl.multiple_of(ys * (px * blk), px * blk), px * blk)
+        v = stg[c, pl.ds(ys * px, px)].reshape(px * blk, cw)
+        o = jnp.dot(wt[0, :, at], v, preferred_element_type=F32) + jnp.dot(
+            wt[1, :, at], v, preferred_element_type=F32
         )
-        pt[lax.rem(c, slots), pl.ds(q * bq, bq)] = o.reshape(bq, tk, cw)
+        o = o.reshape(nz, tk, cw)
+        slot = lax.rem(c, slots)
+
+        @pl.when(q == 0)
+        def _():
+            pt[slot] = o
+
+        @pl.when(q > 0)
+        def _():
+            pt[slot] += o
 
     def sum_send(c, s, dn):
         slot = lax.rem(c, slots)
@@ -426,15 +440,15 @@
 
     sums = []
     for s in range(1, nm + 2):
-        tick = STRIDE * (s - 1)
-        sums.append((3 + tick // py, tick % py, s))
+        tick = STRIDE_SUM * (s - 1)
+        sums.append((LAG + 1 + tick // py, tick % py, s))
     last = nch + max(d for d, _, _ in sums)
 
     def give_back(i, _):
         r = i // py
         q = lax.rem(i, py)
 
-        @pl.when((r == 3) & (q == 0))
+        @pl.when((r == LAG + 1) & (q == 0))
         def _():
             pl.semaphore_wait(credit, 2)
 
@@ -443,25 +457,17 @@
             def _():
                 sum_event(r - d, s)
 
-        @pl.when((q == 0) & (r < 2))
-        def _():
-            wait_d_send(nch - 2 + r)
+        @pl.when((q == 0) & (r < LAG))
+        def _():
+            wait_d_send(nch - LAG + r)
 
         @pl.when(r < nch)
         def _():
             expert_part(r, q)
 
-        @pl.when(r < 2)
-        def _():
-            acc_part(nch - 2 + r, q)
-
-            @pl.when((r == 1) & (q == py - 1))
-            def _():
-                lax.fori_loop(0, cols, backward_act, 0)
-
-        @pl.when((r >= 2) & (r - 2 < nch))
-        def _():
-            combine_part(r - 2, q)
+        @pl.when((r >= LAG) & (r - LAG < nch))
+        def _():
+            combine_part(r - LAG, q)
 
         @pl.when(r < nch)
         def _():
@@ -487,6 +493,14 @@
                 else:
                     remote()
 
+        @pl.when(r < LAG)
+        def _():
+            acc_part(nch - LAG + r, q)
+
+            @pl.when((r == LAG - 1) & (q == py - 1))
+            def _():
+                lax.fori_loop(0, cols, backward_act, 0)
+
         return 0
 
     lax.fori_loop(0, last * py, give_back, 0)
@@ -515,7 +529,7 @@
     cols = py * px
     sl = nz * cap
     blk = el * sl
-    slots = 1 + -(-(STRIDE * (nz // 2)) // py)
+    slots = 1 + -(-(STRIDE_SUM * (nz // 2)) // py)
     half = -(-top // 8) * 8
     pad = ((0, half - top), (0, 0))
     meta = jnp.concatenate(

time: 349 us -> 335 us (0.960)
  Pallas kernels: 341 us -> 325 us
    pallas_call x1, Pallas kernels: 341 us -> 325 us  [on_device(): pl.pallas_call(functools.partial(moe_kernel, cfg), out_shape=(jax.ShapeDt...]
where the time goes in v3:
time: 335 us; the launch traced here: 331 us
  Pallas kernels  325 us (97%)
  local copies, waits for them, and re-layouts  3.36 us (1%)
    pallas_call x1, Pallas kernels, on_device(): pl.pallas_call(functools.partial(moe_kernel, cfg), out_shape=(jax.ShapeDt...  325 us

profile of v3, /device:TPU:32, one launch (start us, length us, event | category | flops | bytes accessed | tf_op | source)
XLA Modules:
  0.0 331.1 jit_solution(7034761649478060532)
XLA Ops:
  0.6 0.7 convert_bitcast_fusion
  1.3 1.3 select_maximum_fusion.meta
  2.6 325.1 %moe.1 = (f32[128,2048]{1,0:T(8,128)}, f32[128,2048]{1,0:T(8,128)}) custom-call(f32[32,128]{1,0:T(8,128)} %select_maximum_fusion.meta, bf16[128,2048]{1,0:T(8,128)(2,1)} %tok.1, bf16[128,2048]{1,0:T(8,128)(2,1)} %cot.1, bf16[2,2048,256]{2,1,0:T(8,128)(2,1)} %wg_hbm.1, bf16[2,2048,256]{2,1,0:T(8,128)(2,1)} %wu_hbm.1, bf16[2,256,2048]{2,1,0:T(8,128)(2,1)} %wd_hbm.1), custom_call_target="tpu_custom_call" | custom-call | tf_op jit(solution)/shard_map/moe/pallas_call | solution.py:541
  327.7 0.0 copy-start
  327.7 2.4 copy.11
  330.1 0.0 copy-done
  330.1 1.0 copy.12
Async XLA Ops:
  327.7 2.4 copy-start

commit v4 on v3

--- a/solution.py
+++ b/solution.py
@@ -21,7 +21,7 @@
 
 
 def moe_kernel(
-    cfg, meta, tok, cot, wg_hbm, wu_hbm, wd_hbm, o_mix, o_grad,
+    cfg, ids_ref, pr_ref, tok, cot, wg_hbm, wu_hbm, wd_hbm, o_mix, o_grad,
     gat, stg, rcv, wg, wu, wd, pm, wt, gu, ga, act, gg, pt, sb, ost, mt,
     l_sem, w_sem, m_send, m_recv, zg_send, zg_recv, d_send, d_recv, d_self,
     r_send, r_recv, r_self, zr_send, zr_recv, o_sem, credit,
@@ -68,6 +68,11 @@
         pltpu.make_async_copy(wd_hbm, wd, w_sem.at[2]),
     ]
 
+    half = mt.shape[1] // 2
+    mt[z] = jnp.zeros_like(mt[z])
+    mt[z, 0:top, :] = ids_ref[...].astype(F32)
+    mt[z, half : half + top, :] = pr_ref[...]
+
     bar = pltpu.get_barrier_semaphore()
 
     def sig_plane(i, _):
@@ -88,7 +93,7 @@
 
     def send_meta(i, _):
         pltpu.make_async_remote_copy(
-            src_ref=meta, dst_ref=mt.at[z], send_sem=m_send.at[i - 1],
+            src_ref=mt.at[z], dst_ref=mt.at[z], send_sem=m_send.at[i - 1],
             recv_sem=m_recv.at[i - 1], device_id=peer(col, lax.rem(z + i, nz)),
             device_id_type=MESH,
         ).start()
@@ -119,13 +124,19 @@
                 gat.at[ch, b], gat.at[ch, b], zg_recv.at[ch, nm + s - 1]
             ).wait()
 
-    def ring_first(ch):
+    def ring_first(ch, far=False):
         pltpu.make_async_copy(gat.at[ch, z], gat.at[ch, z], l_sem.at[ch]).wait()
+        if far:
+            pltpu.make_async_remote_copy(
+                src_ref=gat.at[ch, z], dst_ref=gat.at[ch, z], send_sem=zg_send.at[ch],
+                recv_sem=zg_recv.at[ch, nm - 1], device_id=peer(col, along(nm)),
+                device_id_type=MESH,
+            ).start()
         ring(ch, 1)
 
-    def ring_event(ch, s):
+    def ring_event(ch, s, far=False):
         ring_wait(ch, s)
-        if s < nm:
+        if s < nm - (1 if far else 0):
             ring(ch, s + 1)
 
     steps = [(-1 - STRIDE * (nm - s), s) for s in range(nm + 1)]
@@ -134,11 +145,11 @@
     )
     steps = sorted((t % py, -(t // py), s) for t, s in steps)
 
-    def step(ch, s):
+    def step(ch, s, far=False):
         if s == 0:
-            ring_first(ch)
+            ring_first(ch, far)
         else:
-            ring_event(ch, s)
+            ring_event(ch, s, far)
 
     step(*early[0][1:])
     early = early[1:]
@@ -146,8 +157,6 @@
         own(nc + c, cot, c).start()
     for w in w_copies:
         w.start()
-
-    mt[z] = meta[...]
 
     def wait_meta(i, _):
         pltpu.make_async_copy(mt.at[z], mt.at[z], m_recv.at[i - 1]).wait()
@@ -161,8 +170,6 @@
     eye = (
         lax.broadcasted_iota(jnp.int32, (tk, tk), 0) == lax.broadcasted_iota(jnp.int32, (tk, tk), 1)
     ).astype(F32).astype(BF16)
-    half = mt.shape[1] // 2
-
     def route(b, cnt):
         ids = mt[b, 0:half, :].astype(jnp.int32)
         pr = mt[b, half : 2 * half, :]
@@ -382,17 +389,17 @@
         def _():
             pt[slot] += o
 
-    def sum_send(c, s, dn):
+    def sum_send(c, s, dn, fresh=False, far=False):
         slot = lax.rem(c, slots)
         i = s - 1 if dn else nm + s - 1
         b = along(s - 1 - nm) if dn else along(np_ + 1 - s)
         v = pt[slot, b]
-        if s > 1:
+        if s > 1 and not fresh:
             v = v + gat[c, i - 1].astype(F32)
         sb[slot, i] = v.astype(BF16)
         pltpu.make_async_remote_copy(
             src_ref=sb.at[slot, i], dst_ref=gat.at[c, i], send_sem=zr_send.at[c],
-            recv_sem=zr_recv.at[c, i], device_id=peer(col, zdn if dn else zup),
+            recv_sem=zr_recv.at[c, i], device_id=peer(col, along(-nm) if far else zdn if dn else zup),
             device_id_type=MESH,
         ).start()
 
@@ -403,40 +410,60 @@
         at = pl.ds(pl.multiple_of(c * cw, cw), cw)
         return pltpu.make_async_copy(ost.at[o], dst.at[:, at], o_sem.at[o])
 
+    def finish_sum(c, arrived):
+        total = pt[lax.rem(c, slots), z]
+        for i in arrived:
+            total = total + gat[c, i].astype(F32)
+        o = lax.rem(c, 2)
+
+        @pl.when(c >= 2)
+        def _():
+            out_copy(o_mix, 0, o).wait()
+
+        ost[o] = total
+
+        @pl.when(c < nc)
+        def _():
+            out_copy(o_mix, c, o).start()
+
+        @pl.when(c >= nc)
+        def _():
+            out_copy(o_grad, c - nc, o).start()
+
+        pltpu.make_async_copy(
+            gat.at[c, pl.ds(0, nz - 1)], gat.at[c, pl.ds(0, nz - 1)], zr_send.at[c]
+        ).wait()
+
     def sum_event(c, s):
-        if s > 1:
-            sum_wait(c, s - 2)
-            if s - 1 <= np_:
+        @pl.when(c < nch - 1)
+        def _():
+            if s > 1:
+                sum_wait(c, s - 2)
+                if s - 1 <= np_:
+                    sum_wait(c, nm + s - 2)
+            if s <= nm:
+                sum_send(c, s, True)
+            if s <= np_:
+                sum_send(c, s, False)
+            if s == nm + 1:
+                finish_sum(c, (nm - 1, nm + np_ - 1))
+
+        @pl.when(c == nch - 1)
+        def _():
+            if s == 1:
+                sum_send(c, 2, True, fresh=True)
+                sum_send(c, 1, False)
+                sum_send(c, 1, True, far=True)
+            elif s < nm:
+                sum_wait(c, s - 1)
+                sum_send(c, s + 1, True)
                 sum_wait(c, nm + s - 2)
-        if s <= nm:
-            sum_send(c, s, True)
-        if s <= np_:
-            sum_send(c, s, False)
-        if s == nm + 1:
-            slot = lax.rem(c, slots)
-            total = pt[slot, z] + gat[c, nm - 1].astype(F32)
-            if np_ > 0:
-                total = total + gat[c, nm + np_ - 1].astype(F32)
-
-            o = lax.rem(c, 2)
-
-            @pl.when(c >= 2)
-            def _():
-                out_copy(o_mix, 0, o).wait()
-
-            ost[o] = total
-
-            @pl.when(c < nc)
-            def _():
-                out_copy(o_mix, c, o).start()
-
-            @pl.when(c >= nc)
-            def _():
-                out_copy(o_grad, c - nc, o).start()
-
-            pltpu.make_async_copy(
-                gat.at[c, pl.ds(0, nz - 1)], gat.at[c, pl.ds(0, nz - 1)], zr_send.at[c]
-            ).wait()
+                sum_send(c, s, False)
+            elif s == nm:
+                sum_wait(c, nm - 1)
+                sum_wait(c, nm + np_ - 1)
+                sum_wait(c, 0)
+                finish_sum(c, (nm - 1, nm + np_ - 1, 0))
 
     sums = []
     for s in range(1, nm + 2):
@@ -531,10 +558,6 @@
     blk = el * sl
     slots = 1 + -(-(STRIDE_SUM * (nz // 2)) // py)
     half = -(-top // 8) * 8
-    pad = ((0, half - top), (0, 0))
-    meta = jnp.concatenate(
-        [jnp.pad(expert_ids.T.astype(F32), pad), jnp.pad(probs.T, pad)], axis=0
-    )
     vm = pl.BlockSpec(memory_space=pltpu.VMEM)
     hbm = pl.BlockSpec(memory_space=pl.ANY)
     dma = pltpu.SemaphoreType.DMA
@@ -544,7 +567,7 @@
             jax.ShapeDtypeStruct((tk, dim), F32),
             jax.ShapeDtypeStruct((tk, dim), F32),
         ),
-        in_specs=[vm, hbm, hbm, hbm, hbm, hbm],
+        in_specs=[vm, vm, hbm, hbm, hbm, hbm, hbm],
         out_specs=(hbm, hbm),
         scratch_shapes=[
             pltpu.VMEM((nch, nz, tk, cw), BF16),
@@ -584,7 +607,7 @@
             collective_id=0, has_side_effects=True, vmem_limit_bytes=67043328
         ),
         name="moe",
-    )(meta, tokens, cotangent, gate_weight, up_weight, down_weight)
+    )(expert_ids.T, probs.T, tokens, cotangent, gate_weight, up_weight, down_weight)
 
 
 def solution(mesh):

time: 335 us -> 335 us (level)
  no operation moved by 1% of the time
where the time goes in v4:
time: 335 us; the launch traced here: 330 us
  Pallas kernels  326 us (97%)
  local copies, waits for them, and re-layouts  3.36 us (1%)
    pallas_call x1, Pallas kernels, on_device(): pl.pallas_call(functools.partial(moe_kernel, cfg), out_shape=(jax.ShapeDt...  326 us

profile of v4, /device:TPU:32, one launch (start us, length us, event | category | flops | bytes accessed | tf_op | source)
XLA Modules:
  0.0 330.0 jit_solution(9995590886517338813)
XLA Ops:
  0.6 326.0 %moe.1 = (f32[128,2048]{1,0:T(8,128)}, f32[128,2048]{1,0:T(8,128)}) custom-call(s32[10,128]{1,0:T(8,128)} %bitcast.2, f32[10,128]{1,0:T(8,128)} %bitcast.3, bf16[128,2048]{1,0:T(8,128)(2,1)} %tok.1, bf16[128,2048]{1,0:T(8,128)(2,1)} %cot.1, bf16[2,2048,256]{2,1,0:T(8,128)(2,1)} %wg_hbm.1, bf16[2,2048,256]{2,1,0:T(8,128)(2,1)} %wu_hbm.1, ...), custom_call_target="tpu_custom_call" | custom-call | tf_op jit(solution)/shard_map/moe/pallas_call | solution.py:564
  326.7 0.0 copy-start
  326.7 2.4 copy.11
  329.0 0.0 copy-done
  329.0 1.0 copy.12
Async XLA Ops:
  326.7 2.4 copy-start
